TPU v7x, 512 devices: a whole 4x4x16 slice. The times are simulated.
512 devices in a mesh: row: 32 (over y, z_hi, x), col: 16 (over z_lo, core).
Axes of the slice: x: 4, y: 4, z: 16 (z_hi: 2, z_lo: 8; z = z_hi * 8 + z_lo), core: 2. Of those that a mesh axis runs over, the one named last changes fastest.
Arguments:
- nodes: bfloat16 [2048, 512], P(('row', 'col')), may hold values from -50 to 50
- coords: float32 [3, 2048], P(None, ('row', 'col')), may hold values from -18 to 18
- atom_types: int32 [2048], P(('row', 'col')), may hold values from 0 to 29
- segment_ids: int32 [2048], P(('row', 'col')), may hold values from 0 to 1
- pair_mask: int32 [2048, 2048], P('row', 'col'), may hold values 0 or 1
- pair_bias: bfloat16 [64, 2048, 2048], P(None, 'row', 'col'), may hold values from -10 to 310
- ln_gain: float32 [512], replicated, may hold values from 0.1 to 1.9
- w_qkv: bfloat16 [512, 1536], replicated, may hold values from -0.25 to 0.25
- gauss_mul: float32 [60, 60], replicated, may hold values from 0.25 to 1.75
- gauss_add: float32 [60, 60], replicated, may hold values from -4 to 4
- gauss_mean: float32 [128], replicated, may hold values from 0 to 16
- gauss_width: float32 [128], replicated, may hold values from 0.5 to 2.5
- w_gauss: bfloat16 [128, 128], replicated, may hold values from -2 to 2
- w_heads: bfloat16 [128, 64], replicated, may hold values from -2 to 2
- w_coord1: bfloat16 [64, 64], replicated, may hold values from -0.75 to 0.75
- w_coord2: bfloat16 [64], replicated, may hold values from -0.75 to 0.75
Outputs:
- attended: bfloat16 [2048, 512], P(('row', 'col'))
- moved: float32 [3, 2048], P(None, ('row', 'col'))
All inputs are finite; a program needn't handle non-finite values. No bound on the sum of `pair_mask` on one device may be relied on, other than what follows from the above.
Results may differ from a plain program's by a relative error of at most 0.015.
Values may be sent and summed in bfloat16 or wider, within the bound.
A program may use at most 64 MiB of HBM per device.

v0:
```python
import math

import jax
import jax.numpy as jnp
from jax import lax
from jax.sharding import PartitionSpec as P

ln_epsilon = 1e-05
masked_fill = -1000000000.0
root_shift = 0.01


def combined_all(value, axis, join):
    pieces = jax.tree.map(lambda part: lax.all_gather(part, axis), value)
    head = jax.tree.map(lambda part: part[0], pieces)
    tail = jax.tree.map(lambda part: part[1:], pieces)
    total, _ = lax.scan(lambda total, piece: (join(total, piece), None), head, tail)
    return total


def layer_normed(nodes, ln_gain):
    features = nodes.astype(jnp.float32)
    row_mean = jnp.mean(features, axis=1, keepdims=True)
    centred = features - row_mean
    spread = jnp.mean(centred * centred, axis=1, keepdims=True)
    return (centred * lax.rsqrt(spread + ln_epsilon) * ln_gain[None, :]).astype(jnp.bfloat16)


def gaussians(expanded, gauss_mean, gauss_width):
    scaled = (expanded[None, :, :] - gauss_mean[:, None, None]) / gauss_width[:, None, None]
    norming = math.sqrt(2.0 * math.pi) * gauss_width[:, None, None]
    return (jnp.exp(-0.5 * scaled * scaled) / norming).astype(jnp.bfloat16)


def shards(
    nodes,
    coords,
    atom_types,
    segment_ids,
    pair_mask,
    pair_bias,
    ln_gain,
    w_qkv,
    gauss_mul,
    gauss_add,
    gauss_mean,
    gauss_width,
    w_gauss,
    w_heads,
    w_coord1,
    w_coord2,
):
    col_count = lax.axis_size("col")
    row_count = lax.axis_size("row")
    col_index = lax.axis_index("col")
    row_index = lax.axis_index("row")
    own_rows = nodes.shape[0]
    query_rows = own_rows * col_count
    key_cols = own_rows * row_count
    model_width = nodes.shape[1]
    head_count = pair_bias.shape[0]
    head_dim = model_width // head_count
    kind_count = gauss_mul.shape[0]
    all_atoms = own_rows * row_count * col_count
    highest = lax.Precision.HIGHEST
    normed = layer_normed(nodes, ln_gain)
    kinds = atom_types + kind_count // 2 * segment_ids
    own_table = jnp.concatenate([coords, kinds.astype(jnp.float32)[None, :]], axis=0)
    atom_table = lax.all_gather(own_table, ("row", "col"), axis=1, tiled=True)
    query_table = lax.dynamic_slice_in_dim(atom_table, row_index * query_rows, query_rows, 1)
    key_table = lax.dynamic_slice_in_dim(atom_table, col_index * key_cols, key_cols, 1)
    projected = jnp.dot(
        lax.all_gather(normed, "col", axis=0, tiled=True), w_qkv, preferred_element_type=jnp.float32
    ).astype(jnp.bfloat16)
    queries = projected[:, :model_width].reshape(query_rows, head_count, head_dim)
    row_keys = projected[:, model_width:]
    every_key = lax.all_gather(row_keys, "row", axis=0, tiled=True)
    col_keys = lax.dynamic_slice_in_dim(every_key, col_index * key_cols, key_cols, 0)
    keys_block = col_keys[:, :model_width].reshape(key_cols, head_count, head_dim)
    values_block = col_keys[:, model_width:].reshape(key_cols, head_count, head_dim)
    offsets = query_table[:3, :, None] - key_table[:3, None, :]
    distance = jnp.sqrt(jnp.sum(offsets * offsets, axis=0) + root_shift)
    kind_range = jnp.arange(kind_count, dtype=jnp.float32)
    query_onehot = (query_table[3][:, None] == kind_range[None, :]).astype(jnp.float32)
    key_onehot = (key_table[3][:, None] == kind_range[None, :]).astype(jnp.float32)
    both_tables = jnp.concatenate([gauss_mul, gauss_add], axis=1)
    row_lookup = jnp.dot(query_onehot, both_tables, precision=highest)
    scale_pair = jnp.dot(row_lookup[:, :kind_count], key_onehot.T, precision=highest)
    shift_pair = jnp.dot(row_lookup[:, kind_count:], key_onehot.T, precision=highest)
    expanded = scale_pair * distance + shift_pair
    features = gaussians(expanded, gauss_mean, gauss_width)
    hidden = jax.nn.gelu(
        jnp.einsum("kij,kl->lij", features, w_gauss, preferred_element_type=jnp.float32)
    ).astype(jnp.bfloat16)
    geometry = jnp.einsum("kij,kh->hij", hidden, w_heads, preferred_element_type=jnp.float32)
    affinity = jnp.einsum(
        "ihd,jhd->hij", queries, keys_block, preferred_element_type=jnp.float32
    ) / math.sqrt(head_dim)
    logits = pair_bias.astype(jnp.float32) + geometry + affinity
    pair_new = logits.astype(jnp.bfloat16)
    mixed = jax.nn.gelu(
        jnp.einsum("hij,hg->gij", pair_new, w_coord1, preferred_element_type=jnp.float32)
    ).astype(jnp.bfloat16)
    strength = jnp.einsum("gij,g->ij", mixed, w_coord2, preferred_element_type=jnp.float32)
    strength = jnp.where(pair_mask == 1, strength, 0.0)
    row_total = jnp.sum(strength, axis=1)
    pulled = jnp.dot(strength, key_table[:3].T, precision=highest)
    displace = (query_table[:3].T * row_total[:, None] - pulled) / all_atoms
    masked = jnp.where(pair_mask[None, :, :] == 1, logits, masked_fill)
    local_max = jnp.max(masked, axis=2)

    def join_partial(earlier, later):
        max_early, total_early, sums_early = earlier
        max_late, total_late, sums_late = later
        joined_max = jnp.maximum(max_early, max_late)
        factor_early = jnp.exp(max_early - joined_max)
        factor_late = jnp.exp(max_late - joined_max)
        joined_total = total_early * factor_early + total_late * factor_late
        row_span = sums_early.shape[0]
        joined_sums = (
            sums_early.reshape(row_span, head_count, head_dim) * factor_early.T[:, :, None]
            + sums_late.reshape(row_span, head_count, head_dim) * factor_late.T[:, :, None]
        )
        return (joined_max, joined_total, joined_sums.reshape(row_span, model_width))

    weights = jnp.exp(masked - local_max[:, :, None])
    denominator = jnp.sum(weights, axis=2)
    numerator = jnp.einsum(
        "hij,jhd->ihd",
        weights.astype(jnp.bfloat16),
        values_block,
        preferred_element_type=jnp.float32,
    ).reshape(query_rows, model_width)
    joined_max, joined_total, joined_sums = combined_all(
        (local_max, denominator, numerator), "col", join_partial
    )
    own_sums = lax.dynamic_slice_in_dim(joined_sums, col_index * own_rows, own_rows, 0)
    own_totals = lax.dynamic_slice_in_dim(joined_total, col_index * own_rows, own_rows, 1).T
    own_move = lax.psum_scatter(displace, "col", scatter_dimension=0, tiled=True)
    attended = (
        (own_sums.reshape(own_rows, head_count, head_dim) / own_totals[:, :, None])
        .reshape(own_rows, model_width)
        .astype(jnp.bfloat16)
    )
    moved = coords + own_move.T
    return (attended, moved)


def solution(mesh):
    in_specs = (
        P(("row", "col"), None),
        P(None, ("row", "col")),
        P(("row", "col")),
        P(("row", "col")),
        P("row", "col"),
        P(None, "row", "col"),
        P(),
        P(),
        P(),
        P(),
        P(),
        P(),
        P(),
        P(),
        P(),
        P(),
    )
    out_specs = (P(("row", "col"), None), P(None, ("row", "col")))
    return jax.shard_map(shards, mesh=mesh, in_specs=in_specs, out_specs=out_specs, check_vma=False)
```

profile of v0, /device:TPU:1, one launch (start us, length us, event | category | flops | bytes accessed | tf_op | source)
XLA Modules:
  0.0 1056.8 jit_solution(14597980474348112790)
XLA Ops:
  9.8 37.9 %all-gather.3 = bf16[16,4,512]{2,1,0:T(4,128)(2,1)S(1)} all-gather(bf16[1,4,512]{2,1,0:T(4,128)(2,1)S(1)} %fusion.73), channel_id=1, replica_groups=mesh['row'=32,'col'=16] {'col'}, dimensions={0}, use_global_device_ids=true | all-gather | bytes 69632 | tf_op jit(solution)/shard_map/all_gather | solution.py:73
  49.2 824.8 %all-gather.2 = f32[512,4,4]{2,1,0:T(4,128)S(1)} all-gather(f32[1,4,4]{2,1,0:T(4,128)S(1)} %bitcast.132), channel_id=1, replica_groups=mesh['row'=32,'col'=16] {'row','col'}, dimensions={0}, use_global_device_ids=true | all-gather | bytes 32832 | tf_op jit(solution)/shard_map/all_gather | solution.py:69
  875.1 1.0 fusion.89
  876.4 1.8 fusion.48
  878.2 6.5 fusion.25
  884.7 2.7 fusion.38
  887.5 2.3 select_reduce_fusion
  889.9 1.3 fusion.31
  892.8 1.3 dynamic-slice.2
  894.9 46.2 %all-gather.1 = f32[1024,64]{1,0:T(8,128)S(1)} all-gather(f32[64,64]{1,0:T(8,128)S(1)} %copy.113), channel_id=3, replica_groups=mesh['row'=32,'col'=16] {'col'}, dimensions={0}, use_global_device_ids=true | all-gather | bytes 278528 | tf_op jit(solution)/shard_map/all_gather | solution.py:14
  941.2 29.7 %all-gather = f32[1024,64]{1,0:T(8,128)S(1)} all-gather(f32[64,64]{1,0:T(8,128)S(1)} %copy.112), channel_id=2, replica_groups=mesh['row'=32,'col'=16] {'col'}, dimensions={0}, use_global_device_ids=true | all-gather | bytes 278528 | tf_op jit(solution)/shard_map/all_gather | solution.py:14
  971.0 44.8 %all-reduce = f32[64,3]{0,1:T(4,128)S(1)} all-reduce(f32[64,3]{0,1:T(4,128)S(1)} %fusion.39), channel_id=4, replica_groups=mesh['row'=32,'col'=16] {'col'}, use_global_device_ids=true, to_apply=%region_8.9.clone | all-reduce | flops 192 | bytes 1536
  1016.5 9.0 all-gather.9.cloned.1.call-done
  1026.5 3.0 slice.79
  1029.5 19.2 %while.14 = (s32[]{:T(128)}, f32[64,64]{1,0:T(8,128)S(1)}, f32[64,64]{1,0:T(8,128)S(1)}, f32[64,512]{0,1:T(8,128)S(1)}, f32[15,64,64]{2,1,0:T(8,128)S(1)}, /*ind...) while((s32[]{:T(128)}, f32[64,64]{1,0:T(8,128)S(1)}, f32[64,64]{1,0:T(8,128)S(1)}, ...), condition=%wide.region_6.7_spmd, body=%wide.region_5.6_spmd.sunk | while | flops 126978 | bytes 1163369 | solution.py:17
  1029.6 0.9 constant_dynamic-slice_fusion.5
  1030.9 0.9 constant_dynamic-slice_fusion.5
  1032.2 0.9 constant_dynamic-slice_fusion.5
  1033.5 0.9 constant_dynamic-slice_fusion.5
  1034.8 0.9 constant_dynamic-slice_fusion.5
  1036.0 0.9 constant_dynamic-slice_fusion.5
  1037.3 0.9 constant_dynamic-slice_fusion.5
  1038.6 0.9 constant_dynamic-slice_fusion.5
  1039.9 0.9 constant_dynamic-slice_fusion.5
  (159 shorter events, 20.3 us)
Async XLA Ops:
  7.2 40.6 %copy-start = (bf16[512,1536]{1,0:T(8,128)(2,1)S(1)}, bf16[512,1536]{1,0:T(8,128)(2,1)}, u32[]{:S(2)}) copy-start(bf16[512,1536]{1,0:T(8,128)(2,1)} %param.25) | copy-start | bytes 4718596
  7.2 41.7 %copy-start.10 = (s32[4]{0:T(128)S(1)}, s32[4]{0:T(128)}, u32[]{:S(2)}) copy-start(s32[4]{0:T(128)} %param.21) | copy-start | bytes 52
  7.2 41.7 %copy-start.9 = (s32[4]{0:T(128)S(1)}, s32[4]{0:T(128)}, u32[]{:S(2)}) copy-start(s32[4]{0:T(128)} %param.20) | copy-start | bytes 52
  7.2 41.7 %copy-start.5 = (f32[3,4]{1,0:T(4,128)S(1)}, f32[3,4]{1,0:T(4,128)}, u32[]{:S(2)}) copy-start(f32[3,4]{1,0:T(4,128)} %param.19) | copy-start | bytes 148
  7.2 867.9 %all-gather.7.cloned.1.call-start = ((), (), s32[]{:S(2)}) async-start(), calls=%async_computation | async-start | bytes 4325376 | tf_op jit(solution)/shard_map/all_gather | solution.py:77
  9.8 864.4 %copy-start.11 = (f32[128]{0:T(128)S(1)}, f32[128]{0:T(128)}, u32[]{:S(2)}) copy-start(f32[128]{0:T(128)} %param.29) | copy-start | bytes 1540
  9.8 864.5 %copy-start.2 = (f32[60,60]{1,0:T(8,128)S(1)}, f32[60,60]{1,0:T(8,128)}, u32[]{:S(2)}) copy-start(f32[60,60]{1,0:T(8,128)} %param.27) | copy-start | bytes 43204
  9.8 864.5 %copy-start.3 = (f32[60,60]{1,0:T(8,128)S(1)}, f32[60,60]{1,0:T(8,128)}, u32[]{:S(2)}) copy-start(f32[60,60]{1,0:T(8,128)} %param.26) | copy-start | bytes 43204
  48.8 976.7 %all-gather.9.cloned.1.call-start = ((), (), s32[]{:S(2)}) async-start(), calls=%async_computation.1 | async-start | bytes 2228224 | tf_op jit(solution)/shard_map/all_gather | solution.py:14
  874.0 4.2 copy-start.6
  874.0 4.2 copy-start.7
  874.0 4.2 copy-start.12
  878.2 6.5 copy-start.8
  878.2 6.5 copy-start.13
  884.7 2.7 copy-start.4
  887.4 2.5 copy-start.1
Sparse Core Ops, SparseCore 0:
  48.9 166.9 all-gather.6
  892.9 132.4 all-gather.8
where the time goes:
time: 1060 us
  blocking collectives  983 us (93%)
  local copies, waits for them, and re-layouts  24.8 us (2%)
  between operations  15 us (1%)
  matrix products  13.1 us (1%)
  other arithmetic  10.6 us (1%)
    all_gather x1, blocking collectives, shards(): atom_table = lax.all_gather(own_table, ('row', 'col'), axis=1, tiled=True)  825 us
    all_gather x2, blocking collectives, combined_all(): pieces = jax.tree.map(lambda part: lax.all_gather(part, axis), value)  75.9 us
    unnamed x1, blocking collectives  44.8 us
    all_gather x1, blocking collectives, shards(): lax.all_gather(normed, 'col', axis=0, tiled=True)  37.9 us
  transfers between devices with their start and end apart: 2, of which 1 were waited for; matrix products, arithmetic and copies ran while one was open for 0% of the time, Pallas kernels for 0%

commit v1 on v0

v1 whole, which is shorter than its diff:
```python
import functools
import math

import jax
import jax.numpy as jnp
from jax import lax
from jax.experimental import pallas as pl
from jax.experimental.pallas import tpu as pltpu
from jax.sharding import PartitionSpec as P

MESH = pl.DeviceIdType.MESH
F32 = jnp.float32
BF16 = jnp.bfloat16
ln_epsilon = 1e-05
masked_fill = -1000000000.0
root_shift = 0.01
GELU_A = math.sqrt(2.0 / math.pi)
GELU_B = GELU_A * 0.044715


def gelu(x):
    half = 0.5 * x
    return half + half * jnp.tanh(x * (GELU_A + GELU_B * (x * x)))


def nt_dot(a, b):
    return lax.dot_general(a, b, (((1,), (1,)), ((), ())), preferred_element_type=F32)


def nn_dot(a, b, precision=None):
    return jnp.dot(a, b, preferred_element_type=F32, precision=precision)


def lanes(shape):
    return lax.broadcasted_iota(jnp.int32, shape, len(shape) - 1)


def layer_norm(nodes, gain):
    x = nodes.astype(F32)
    centred = x - jnp.mean(x, axis=1, keepdims=True)
    spread = jnp.mean(centred * centred, axis=1, keepdims=True)
    return (centred * lax.rsqrt(spread + ln_epsilon) * gain).astype(BF16)


def prepare(w):
    w.wg_t[...] = w.w_gauss[...].astype(F32).T.astype(BF16)
    w.w1_t[...] = w.w_coord1[...].astype(F32).T.astype(BF16)
    w2 = w.w_coord2[...].astype(F32)
    wide = jnp.concatenate([w2] * 8, axis=1)
    own = lanes((8, 512)) // 64 == lax.broadcasted_iota(jnp.int32, (8, 512), 0)
    w.w2_b[...] = jnp.where(own, jnp.broadcast_to(wide, (8, 512)), 0.0).astype(BF16)
    mean = jnp.broadcast_to(w.gauss_mean[...], (128, 128)).T
    width = jnp.broadcast_to(w.gauss_width[...], (128, 128)).T
    slope = math.sqrt(0.5 * math.log2(math.e)) / width
    w.g_a[...] = slope
    w.g_b[...] = slope * mean
    w.g_c[...] = -jnp.log2(math.sqrt(2.0 * math.pi) * width)


def joined(parts):
    return parts + pltpu.roll(parts, 120, 1) + pltpu.roll(parts, 112, 1)


def pair_distances(w):
    for s in range(w.q_nodes.shape[0]):
        w.q_f[4 * s : 4 * s + 4, :] = w.q_nodes[s].astype(F32)
    for s in range(w.k_nodes.shape[0]):
        w.k_f[4 * s : 4 * s + 4, :] = w.k_nodes[s].astype(F32)
    qt = joined(w.q_f[:, 512:640])
    w.q_t[...] = qt
    kt = joined(w.k_f[:, 512:640]).T
    w.k_row[...] = kt[0:8, :]
    total = root_shift
    for axis in range(3):
        offset = qt[:, axis : axis + 1] - kt[axis : axis + 1, :]
        total = total + offset * offset
    distance = jnp.sqrt(total)
    kinds = w.gauss_mul.shape[0]
    q_hot = (lanes((64, kinds)).astype(F32) == qt[:, 3:4]).astype(F32)
    k_hot = (lax.broadcasted_iota(jnp.int32, (kinds, 128), 0).astype(F32) == kt[3:4, :]).astype(F32)
    high = lax.Precision.HIGHEST
    scale = nn_dot(nn_dot(q_hot, w.gauss_mul[...], high), k_hot, high)
    shift = nn_dot(nn_dot(q_hot, w.gauss_add[...], high), k_hot, high)
    w.expanded[...] = scale * distance + shift


def geometry(w):
    step = 8

    def chunk(c, carry):
        base = pl.multiple_of(c * step, step)
        rows = w.expanded[pl.ds(base, step), :]
        a, b, k = w.g_a[...], w.g_b[...], w.g_c[...]
        parts = []
        for i in range(step):
            t = a * rows[i : i + 1, :] - b
            parts.append(jnp.exp2(k - t * t).astype(BF16))
        features = jnp.concatenate(parts, axis=1)
        hidden = gelu(nn_dot(w.wg_t[...], features)).astype(BF16)
        geo = nn_dot(w.w_heads[...], hidden)
        for i in range(step):
            w.logits[pl.ds(base + i, 64, stride=64), :] = geo[:, 128 * i : 128 * i + 128]
        return carry

    lax.fori_loop(0, 64 // step, chunk, 0)


def project(w):
    qn = w.q_f[:, 0:512].astype(BF16)
    kn = w.k_f[:, 0:512].astype(BF16)
    w.q_p[...] = nn_dot(qn, w.w_qkv[:, 0:512]).astype(BF16)
    w.k_p[...] = nn_dot(kn, w.w_qkv[:, 512:1024]).astype(BF16)
    w.v_p[...] = nn_dot(kn, w.w_qkv[:, 1024:1536]).astype(BF16)


def attention(w):
    take = w.mask[...] == 1
    lane = lanes((64, 128))
    ones = jnp.ones((128, 128), BF16)
    scale = 1.0 / math.sqrt(8.0)
    per = 4
    maxima = jnp.zeros((64, 128), F32)
    totals = jnp.ones((64, 128), F32)
    for g in range(4):
        cols = slice(128 * g, 128 * g + 128)
        q_g = w.q_p[:, cols].astype(F32)
        k_g = w.k_p[:, cols]
        v_g = jnp.concatenate([w.v_p[:, cols], ones], axis=1)

        def heads(n, carry, g=g, q_g=q_g, k_g=k_g, v_g=v_g):
            maxima, totals, num, den = carry
            sel = [(lane >> 3) == n * per + u for u in range(per)]
            left = jnp.concatenate([jnp.where(s, q_g, 0.0).astype(BF16) for s in sel], axis=0)
            affinity = nt_dot(left, k_g)
            probs = []
            tops = []
            for u in range(per):
                head = g * 16 + n * per + u
                at = pl.ds(pl.multiple_of(head * 64, 64), 64)
                logit = (
                    w.bias[head].astype(F32)
                    + w.logits[at, :]
                    + affinity[64 * u : 64 * u + 64] * scale
                )
                w.logits[at, :] = logit
                masked = jnp.where(take, logit, masked_fill)
                top = jnp.max(masked, axis=1, keepdims=True)
                tops.append(top)
                probs.append(jnp.exp(masked - top).astype(BF16))
            out = nn_dot(jnp.concatenate(probs, axis=0), v_g)
            for u in range(per):
                head = g * 16 + n * per + u
                part = out[64 * u : 64 * u + 64]
                num = jnp.where(sel[u], part[:, 0:128], num)
                den = jnp.where(sel[u], part[:, 128:256], den)
                here = lane == head
                maxima = jnp.where(here, tops[u], maxima)
                totals = jnp.where(here, part[:, 128:256], totals)
            return maxima, totals, num, den

        zero = jnp.zeros((64, 128), F32)
        maxima, totals, num, den = lax.fori_loop(0, 16 // per, heads, (maxima, totals, zero, zero))
        part = num / den
        for s in range(16):
            w.att_s[s, :, cols] = part[4 * s : 4 * s + 4].astype(BF16)
    stat = maxima + jnp.log(totals)
    for s in range(16):
        w.lse_s[s] = stat[4 * s : 4 * s + 4]


def displacement(w):
    step = 8

    def chunk(c, carry):
        base = pl.multiple_of(c * step, step)
        parts = [w.logits[pl.ds(base + i, 64, stride=64), :].astype(BF16) for i in range(step)]
        mixed = gelu(nn_dot(w.w1_t[...], jnp.concatenate(parts, axis=1))).astype(BF16)
        stacked = jnp.concatenate([mixed[:, 128 * i : 128 * i + 128] for i in range(step)], axis=0)
        w.strength[pl.ds(base, step), :] = nn_dot(w.w2_b[...], stacked)
        return carry

    lax.fori_loop(0, 64 // step, chunk, 0)
    strength = jnp.where(w.mask[...] == 1, w.strength[...], 0.0)
    qt = w.q_t[...]
    lane = lanes((64, 128))
    out = jnp.zeros((64, 128), F32)
    for axis in range(3):
        offset = qt[:, axis : axis + 1] - w.k_row[axis : axis + 1, :]
        moved = jnp.sum(strength * offset, axis=1, keepdims=True) * (1.0 / w.atoms)
        out = jnp.where(lane == axis, moved, out)
    for s in range(16):
        w.dis_s[s] = out[4 * s : 4 * s + 4]


def combine_attended(w):
    count = 16
    top = w.lse_r[0]
    for s in range(1, count):
        top = jnp.maximum(top, w.lse_r[s])
    total = jnp.zeros((4, 128), F32)
    for s in range(count):
        e = jnp.exp(w.lse_r[s] - top)
        w.coef[4 * s : 4 * s + 4, :] = e
        total = total + e
    inverse = 1.0 / total
    for s in range(count):
        w.coef[4 * s : 4 * s + 4, :] = w.coef[4 * s : 4 * s + 4, :] * inverse
    spread = (lanes((128, 512)) // 8 == lax.broadcasted_iota(jnp.int32, (128, 512), 0)).astype(BF16)
    coef = w.coef[...]
    top_part = coef.astype(BF16)
    rest = (coef - top_part.astype(F32)).astype(BF16)
    w.q_f[:, 0:512] = nn_dot(top_part, spread) + nn_dot(rest, spread)
    result = jnp.zeros((4, 512), F32)
    for s in range(count):
        result = result + w.q_f[4 * s : 4 * s + 4, 0:512] * w.att_r[s].astype(F32)
    return result.astype(BF16)


def combine_moved(w):
    total = w.dis_r[0]
    for s in range(1, 16):
        total = total + w.dis_r[s]
    w.pad[0:4, :] = total
    w.pad_t[...] = w.pad[...].T
    return w.coords[...] + w.pad_t[0:3, 0:4]


LOADED = dict(
    nodes=((4, 512), BF16),
    coords=((3, 4), F32),
    types=((1, 4), jnp.int32),
    segments=((1, 4), jnp.int32),
    ln_gain=((1, 512), F32),
    gauss_mean=((1, 128), F32),
    gauss_width=((1, 128), F32),
    w_gauss=((128, 128), BF16),
    w_coord1=((64, 64), BF16),
    w_coord2=((1, 64), BF16),
    gauss_mul=((60, 60), F32),
    gauss_add=((60, 60), F32),
    w_heads=((64, 128), BF16),
    mask=((64, 128), jnp.int32),
    w_qkv=((512, 1536), BF16),
    bias=((64, 64, 128), BF16),
)
WORK = dict(
    wg_t=((128, 128), BF16),
    w1_t=((64, 64), BF16),
    w2_b=((8, 512), BF16),
    g_a=((128, 128), F32),
    g_b=((128, 128), F32),
    g_c=((128, 128), F32),
    q_t=((64, 128), F32),
    k_row=((8, 128), F32),
    expanded=((64, 128), F32),
    logits=((4096, 128), F32),
    q_f=((64, 640), F32),
    k_f=((128, 640), F32),
    q_p=((64, 512), BF16),
    k_p=((128, 512), BF16),
    v_p=((128, 512), BF16),
    strength=((64, 128), F32),
    coef=((64, 128), F32),
    pad=((128, 128), F32),
    pad_t=((128, 128), F32),
    own=((4, 640), BF16),
    q_nodes=((16, 4, 640), BF16),
    k_nodes=((32, 4, 640), BF16),
    att_s=((16, 4, 512), BF16),
    lse_s=((16, 4, 128), F32),
    dis_s=((16, 4, 128), F32),
    att_r=((16, 4, 512), BF16),
    lse_r=((16, 4, 128), F32),
    dis_r=((16, 4, 128), F32),
)


class Refs:
    pass


def own_block(w):
    w.own[:, 0:512] = layer_norm(w.nodes[...], w.ln_gain[...])
    w.pad[...] = jnp.zeros((128, 128), F32)
    rest = w.coords[...]
    for part in range(3):
        piece = rest.astype(BF16).astype(F32)
        w.pad[8 * part : 8 * part + 3, 0:4] = piece
        rest = rest - piece
    kinds = w.types[...] + w.gauss_mul.shape[0] // 2 * w.segments[...]
    w.pad[3:4, 0:4] = kinds.astype(F32)
    w.pad_t[...] = w.pad[...].T
    w.own[:, 512:640] = w.pad_t[0:4, :].astype(BF16)


def kernel(rows, cols, *refs):
    w = Refs()
    count = len(LOADED)
    sources, refs = refs[:count], refs[count:]
    w.attended, w.moved = refs[:2]
    refs = refs[2:]
    for name, ref in zip([*LOADED, *WORK], refs):
        setattr(w, name, ref)
    load_sem, kz_send, kz_recv, kx_send, kx_recv, qn_send, qn_recv = refs[-13:-6]
    at_send, at_recv, ls_send, ls_recv, ds_send, ds_recv = refs[-6:]
    w.atoms = float(rows * cols * 4)
    row, col = lax.axis_index("row"), lax.axis_index("col")
    x, line = lax.rem(row, 4), lax.rem(row // 4, 2)
    level, core = col // 2, lax.rem(col, 2)
    home = row // 2
    own_key = home == col
    relay = core == x // 2
    half = lax.rem(x, 2)
    planes = rows // 4
    source_row = level * 4 + x

    def with_x(other):
        return row - x + other

    barrier = pltpu.get_barrier_semaphore()

    def greet(r, c):
        pl.semaphore_signal(barrier, inc=1, device_id=(r, c), device_id_type=MESH)

    def greet_row(n, carry):
        greet(row, lax.rem(col + n, cols))
        return carry

    @pl.when(relay)
    def _():
        def greet_source(n, carry):
            @pl.when(jnp.logical_not(jnp.logical_and(source_row == row, n == col)))
            def _():
                greet(source_row, n)

            return carry

        lax.fori_loop(0, cols, greet_source, 0)

    lax.fori_loop(1, cols, greet_row, 0)
    for side in range(2):
        other = 2 * core + side

        @pl.when(other != x)
        def _(other=other):
            greet(with_x(other), col)

    loads = []
    for n, (name, source) in enumerate(zip(LOADED, sources, strict=True)):
        loads.append(pltpu.make_async_copy(source, getattr(w, name), load_sem.at[n]))
        loads[-1].start()
    for load in loads[:-2]:
        load.wait()
    own_block(w)
    prepare(w)

    pl.semaphore_wait(
        barrier, cols - 1 + planes - jnp.where(own_key, 1, 0) + jnp.where(relay, 3, 0)
    )

    def far_copy(n):
        plane = lax.rem(row // 4 + n, planes)
        return pltpu.make_async_remote_copy(
            src_ref=w.own,
            dst_ref=w.k_nodes.at[half * cols + col],
            send_sem=kz_send.at[n],
            recv_sem=kz_recv.at[col],
            device_id=(plane * 4 + x, home),
            device_id_type=MESH,
        )

    def far_copies(act):
        def one(n, carry):
            act(far_copy(n))
            return carry

        lax.fori_loop(1, planes, one, 0)

        @pl.when(jnp.logical_not(own_key))
        def _():
            act(far_copy(0))

    def relay_copy(pair, step):
        part = w.k_nodes.at[pl.ds(half * cols + 2 * pair, 2)]
        return pltpu.make_async_remote_copy(
            src_ref=part,
            dst_ref=part,
            send_sem=kx_send.at[pair * 3 + step - 1],
            recv_sem=kx_recv.at[half * (cols // 2) + pair],
            device_id=(with_x(lax.rem(x + step, 4)), col),
            device_id_type=MESH,
        )

    def row_copy(src, dst, send, recv, n):
        c = lax.rem(col + n, cols)
        return pltpu.make_async_remote_copy(
            src_ref=src(c),
            dst_ref=dst.at[col],
            send_sem=send.at[n],
            recv_sem=recv.at[col],
            device_id=(row, c),
            device_id_type=MESH,
        )

    def row_copies(src, dst, send, recv, act):
        def one(n, carry):
            act(row_copy(src, dst, send, recv, n))
            return carry

        lax.fori_loop(1, cols, one, 0)

    def start(copy):
        copy.start()

    def sent(copy):
        copy.wait_send()

    def wait_row(src, dst, recv):
        def one(n, carry):
            c = lax.rem(col + n, cols)
            pltpu.make_async_copy(src(c), dst.at[c], recv.at[c]).wait()
            return carry

        lax.fori_loop(1, cols, one, 0)

    nod = lambda c: w.own
    far_copies(start)
    row_copies(nod, w.q_nodes, qn_send, qn_recv, start)
    w.q_nodes[col] = w.own[...]

    @pl.when(own_key)
    def _():
        w.k_nodes[half * cols + col] = w.own[...]

    @pl.when(relay)
    def _():
        def forward(n, carry):
            pair = lax.rem(level + 1 + n, cols // 2)
            for side in range(2):
                c = 2 * pair + side

                @pl.when(jnp.logical_not(jnp.logical_and(own_key, c == col)))
                def _(c=c):
                    into = w.k_nodes.at[half * cols + c]
                    pltpu.make_async_copy(w.own, into, kz_recv.at[c]).wait()

            for step in range(1, 4):
                relay_copy(pair, step).start()
            return carry

        lax.fori_loop(0, cols // 2, forward, 0)

    wait_row(nod, w.q_nodes, qn_recv)
    for side in range(2):

        @pl.when(jnp.logical_not(jnp.logical_and(relay, half == side)))
        def _(side=side):
            def arrive(pair, carry):
                part = w.k_nodes.at[pl.ds(side * cols + 2 * pair, 2)]
                pltpu.make_async_copy(part, part, kx_recv.at[side * (cols // 2) + pair]).wait()
                return carry

            lax.fori_loop(0, cols // 2, arrive, 0)

    pair_distances(w)
    geometry(w)
    for load in loads[-2:]:
        load.wait()
    project(w)
    attention(w)
    att = lambda c: w.att_s.at[c]
    lse = lambda c: w.lse_s.at[c]
    dis = lambda c: w.dis_s.at[c]
    row_copies(att, w.att_r, at_send, at_recv, start)
    row_copies(lse, w.lse_r, ls_send, ls_recv, start)
    w.att_r[col] = w.att_s[col]
    w.lse_r[col] = w.lse_s[col]
    displacement(w)
    row_copies(dis, w.dis_r, ds_send, ds_recv, start)
    w.dis_r[col] = w.dis_s[col]
    far_copies(sent)
    row_copies(nod, w.q_nodes, qn_send, qn_recv, sent)

    @pl.when(relay)
    def _():
        def drain(n, carry):
            for step in range(1, 4):
                relay_copy(n, step).wait_send()
            return carry

        lax.fori_loop(0, cols // 2, drain, 0)

    row_copies(att, w.att_r, at_send, at_recv, sent)
    row_copies(lse, w.lse_r, ls_send, ls_recv, sent)
    wait_row(att, w.att_r, at_recv)
    wait_row(lse, w.lse_r, ls_recv)
    w.attended[...] = combine_attended(w)
    row_copies(dis, w.dis_r, ds_send, ds_recv, sent)
    wait_row(dis, w.dis_r, ds_recv)
    w.moved[...] = combine_moved(w)


def shards(
    nodes,
    coords,
    atom_types,
    segment_ids,
    pair_mask,
    pair_bias,
    ln_gain,
    w_qkv,
    gauss_mul,
    gauss_add,
    gauss_mean,
    gauss_width,
    w_gauss,
    w_heads,
    w_coord1,
    w_coord2,
    *,
    rows,
    cols,
):
    vmem = pl.BlockSpec(memory_space=pltpu.VMEM)
    hbm = pl.BlockSpec(memory_space=pl.ANY)
    dma = lambda n: pltpu.SemaphoreType.DMA((n,))
    return pl.pallas_call(
        functools.partial(kernel, rows, cols),
        out_shape=(
            jax.ShapeDtypeStruct(nodes.shape, BF16),
            jax.ShapeDtypeStruct(coords.shape, F32),
        ),
        in_specs=[hbm] * len(LOADED),
        out_specs=(vmem, vmem),
        scratch_shapes=[pltpu.VMEM(*spec) for spec in [*LOADED.values(), *WORK.values()]]
        + [dma(len(LOADED)), dma(rows // 4), dma(cols), dma(3 * cols // 2), dma(cols)]
        + [dma(cols)] * 8,
        compiler_params=pltpu.CompilerParams(collective_id=0, has_side_effects=True),
        name="refine",
    )(
        nodes,
        coords,
        atom_types[None],
        segment_ids[None],
        ln_gain[None],
        gauss_mean[None],
        gauss_width[None],
        w_gauss,
        w_coord1,
        w_coord2[None],
        gauss_mul,
        gauss_add,
        w_heads.T,
        pair_mask,
        w_qkv,
        pair_bias,
    )


def solution(mesh):
    in_specs = (
        P(("row", "col"), None),
        P(None, ("row", "col")),
        P(("row", "col")),
        P(("row", "col")),
        P("row", "col"),
        P(None, "row", "col"),
    ) + (P(),) * 10
    out_specs = (P(("row", "col"), None), P(None, ("row", "col")))
    body = functools.partial(shards, rows=mesh.shape["row"], cols=mesh.shape["col"])
    return jax.shard_map(body, mesh=mesh, in_specs=in_specs, out_specs=out_specs, check_vma=False)
```

time: 1060 us -> 56.4 us (0.05)
  blocking collectives: 983 us -> 0 us
  Pallas kernels: 0 us -> 53.1 us
  local copies, waits for them, and re-layouts: 24.8 us -> 2.5 us
  between operations: 15 us -> 0.65 us
  matrix products: 13.1 us -> 0 us
  other arithmetic: 10.6 us -> 0 us
    all_gather x4 -> x0, blocking collectives: 939 us -> none  [the longest x1 825 us: shards(): atom_table = lax.all_gather(own_table, ('row', 'col'), axis=1, tiled=True)]
    pallas_call x0 -> x1, Pallas kernels: none -> 53.1 us  [shards(): pl.pallas_call(functools.partial(kernel, rows, cols), out_shape=(jax.Shap...]
    unnamed x1 -> x0, blocking collectives: 44.8 us -> none
    dynamic_slice x30 -> x0, local copies, waits for them, and re-layouts: 15.6 us -> none  [combined_all(): lax.scan(lambda total, piece: (join(total, piece), None), head, tail)]
    dot_general x9 -> x0, matrix products: 13.1 us -> none  [the longest x1 6.51 us: shards(): jnp.einsum('kij,kh->hij', hidden, w_heads, preferred_element_type=jnp.flo...]
  transfers between devices with their start and end apart: 2 -> 0, of which waited for: 1 -> 0; matrix products, arithmetic and copies ran while one was open for 0% -> 0% of each run, Pallas kernels for 0% -> 0%
where the time goes in v1:
time: 56.4 us; the launch traced here: 56.2 us
  Pallas kernels  53.1 us (94%)
  local copies, waits for them, and re-layouts  2.5 us (4%)
  between operations  0.65 us (1%)
    pallas_call x1, Pallas kernels, shards(): pl.pallas_call(functools.partial(kernel, rows, cols), out_shape=(jax.Shap...  53.1 us
    unnamed x2, local copies, waits for them, and re-layouts  2.5 us

profile of v1, /device:TPU:1, one launch (start us, length us, event | category | flops | bytes accessed | tf_op | source)
XLA Modules:
  0.0 56.2 jit_solution(2452184552622008133)
XLA Ops:
  0.6 53.1 %refine.1 = (bf16[4,512]{1,0:T(4,128)(2,1)}, f32[3,4]{1,0:T(4,128)}) custom-call(bf16[4,512]{1,0:T(4,128)(2,1)} %refs_0_.1, f32[3,4]{1,0:T(4,128)} %refs_1_.1, s32[1,4]{1,0:T(1,128)} %bitcast.9, s32[1,4]{1,0:T(1,128)} %bitcast.10, f32[1,512]{1,0:T(1,128)} %bitcast.8, f32[1,128]{1,0:T(1,128)} %bitcast.11, f32[1,128]{1,0:T(1,128)} %bitcast.12, ...), custom_call_target="tpu_custom_call" | custom-call | tf_op jit(solution)/shard_map/refine/pallas_call | solution.py:527
  53.7 1.3 %copy.20 = bf16[4,512]{1,0:T(4,128)(2,1)} copy(bf16[4,512]{1,0:T(4,128)(2,1)} %get-tuple-element.4) | data formatting | bytes 8192
  55.0 1.2 %copy.21 = f32[3,4]{1,0:T(4,128)} copy(f32[3,4]{1,0:T(4,128)} %get-tuple-element.5) | data formatting | bytes 96

commit v2 on v1

--- a/solution.py
+++ b/solution.py
@@ -84,25 +84,18 @@
     w.expanded[...] = scale * distance + shift
 
 
-def geometry(w):
-    step = 8
-
-    def chunk(c, carry):
-        base = pl.multiple_of(c * step, step)
-        rows = w.expanded[pl.ds(base, step), :]
-        a, b, k = w.g_a[...], w.g_b[...], w.g_c[...]
-        parts = []
-        for i in range(step):
+def geometry(w, q, logits):
+    a, b, k = w.g_a[...], w.g_b[...], w.g_c[...]
+    for part in range(2):
+        rows = w.expanded[pl.ds(pl.multiple_of(16 * q + 8 * part, 8), 8), :]
+        pieces = []
+        for i in range(8):
             t = a * rows[i : i + 1, :] - b
-            parts.append(jnp.exp2(k - t * t).astype(BF16))
-        features = jnp.concatenate(parts, axis=1)
-        hidden = gelu(nn_dot(w.wg_t[...], features)).astype(BF16)
+            pieces.append(jnp.exp2(k - t * t).astype(BF16))
+        hidden = gelu(nn_dot(w.wg_t[...], jnp.concatenate(pieces, axis=1))).astype(BF16)
         geo = nn_dot(w.w_heads[...], hidden)
-        for i in range(step):
-            w.logits[pl.ds(base + i, 64, stride=64), :] = geo[:, 128 * i : 128 * i + 128]
-        return carry
-
-    lax.fori_loop(0, 64 // step, chunk, 0)
+        for i in range(8):
+            logits[pl.ds(8 * part + i, 64, stride=16), :] = geo[:, 128 * i : 128 * i + 128]
 
 
 def project(w):
@@ -113,83 +106,59 @@
     w.v_p[...] = nn_dot(kn, w.w_qkv[:, 1024:1536]).astype(BF16)
 
 
-def attention(w):
-    take = w.mask[...] == 1
-    lane = lanes((64, 128))
+def attention(w, q, logits):
+    here = pl.ds(pl.multiple_of(16 * q, 16), 16)
+    take = (w.mask[here, :] == 1)[None]
+    lane = lanes((16, 128))
+    own = [(lane >> 3) == head for head in range(16)]
     ones = jnp.ones((128, 128), BF16)
     scale = 1.0 / math.sqrt(8.0)
-    per = 4
-    maxima = jnp.zeros((64, 128), F32)
-    totals = jnp.ones((64, 128), F32)
+    maxima = jnp.zeros((16, 128), F32)
+    totals = jnp.ones((16, 128), F32)
     for g in range(4):
         cols = slice(128 * g, 128 * g + 128)
-        q_g = w.q_p[:, cols].astype(F32)
-        k_g = w.k_p[:, cols]
-        v_g = jnp.concatenate([w.v_p[:, cols], ones], axis=1)
-
-        def heads(n, carry, g=g, q_g=q_g, k_g=k_g, v_g=v_g):
-            maxima, totals, num, den = carry
-            sel = [(lane >> 3) == n * per + u for u in range(per)]
-            left = jnp.concatenate([jnp.where(s, q_g, 0.0).astype(BF16) for s in sel], axis=0)
-            affinity = nt_dot(left, k_g)
-            probs = []
-            tops = []
-            for u in range(per):
-                head = g * 16 + n * per + u
-                at = pl.ds(pl.multiple_of(head * 64, 64), 64)
-                logit = (
-                    w.bias[head].astype(F32)
-                    + w.logits[at, :]
-                    + affinity[64 * u : 64 * u + 64] * scale
-                )
-                w.logits[at, :] = logit
-                masked = jnp.where(take, logit, masked_fill)
-                top = jnp.max(masked, axis=1, keepdims=True)
-                tops.append(top)
-                probs.append(jnp.exp(masked - top).astype(BF16))
-            out = nn_dot(jnp.concatenate(probs, axis=0), v_g)
-            for u in range(per):
-                head = g * 16 + n * per + u
-                part = out[64 * u : 64 * u + 64]
-                num = jnp.where(sel[u], part[:, 0:128], num)
-                den = jnp.where(sel[u], part[:, 128:256], den)
-                here = lane == head
-                maxima = jnp.where(here, tops[u], maxima)
-                totals = jnp.where(here, part[:, 128:256], totals)
-            return maxima, totals, num, den
-
-        zero = jnp.zeros((64, 128), F32)
-        maxima, totals, num, den = lax.fori_loop(0, 16 // per, heads, (maxima, totals, zero, zero))
+        rows = slice(256 * g, 256 * g + 256)
+        q_g = w.q_p[here, cols].astype(F32)
+        left = jnp.concatenate([jnp.where(o, q_g, 0.0).astype(BF16) for o in own], axis=0)
+        bias = w.bias[16 * g : 16 * g + 16, here, :].astype(F32).reshape(256, 128)
+        logit = bias + logits[rows, :] + nt_dot(left, w.k_p[:, cols]) * scale
+        logits[rows, :] = logit
+        masked = jnp.where(take, logit.reshape(16, 16, 128), masked_fill)
+        top = jnp.max(masked, axis=2, keepdims=True)
+        probs = jnp.exp(masked - top).astype(BF16).reshape(256, 128)
+        out = nn_dot(probs, jnp.concatenate([w.v_p[:, cols], ones], axis=1))
+        num = jnp.zeros((16, 128), F32)
+        den = jnp.ones((16, 128), F32)
+        for head in range(16):
+            part = out[16 * head : 16 * head + 16]
+            num = jnp.where(own[head], part[:, 0:128], num)
+            den = jnp.where(own[head], part[:, 128:256], den)
+            column = lane == 16 * g + head
+            maxima = jnp.where(column, top[head], maxima)
+            totals = jnp.where(column, part[:, 128:256], totals)
         part = num / den
-        for s in range(16):
-            w.att_s[s, :, cols] = part[4 * s : 4 * s + 4].astype(BF16)
-    stat = maxima + jnp.log(totals)
-    for s in range(16):
-        w.lse_s[s] = stat[4 * s : 4 * s + 4]
-
-
-def displacement(w):
-    step = 8
-
-    def chunk(c, carry):
-        base = pl.multiple_of(c * step, step)
-        parts = [w.logits[pl.ds(base + i, 64, stride=64), :].astype(BF16) for i in range(step)]
+        for s in range(4):
+            w.att_s[4 * q + s, :, cols] = part[4 * s : 4 * s + 4].astype(BF16)
+    return maxima + jnp.log(totals)
+
+
+def displacement(w, q, logits, stat):
+    here = pl.ds(pl.multiple_of(16 * q, 16), 16)
+    pieces = []
+    for part in range(2):
+        parts = [logits[pl.ds(8 * part + i, 64, stride=16), :].astype(BF16) for i in range(8)]
         mixed = gelu(nn_dot(w.w1_t[...], jnp.concatenate(parts, axis=1))).astype(BF16)
-        stacked = jnp.concatenate([mixed[:, 128 * i : 128 * i + 128] for i in range(step)], axis=0)
-        w.strength[pl.ds(base, step), :] = nn_dot(w.w2_b[...], stacked)
-        return carry
-
-    lax.fori_loop(0, 64 // step, chunk, 0)
-    strength = jnp.where(w.mask[...] == 1, w.strength[...], 0.0)
-    qt = w.q_t[...]
-    lane = lanes((64, 128))
-    out = jnp.zeros((64, 128), F32)
+        stacked = jnp.concatenate([mixed[:, 128 * i : 128 * i + 128] for i in range(8)], axis=0)
+        pieces.append(nn_dot(w.w2_b[...], stacked))
+    strength = jnp.where(w.mask[here, :] == 1, jnp.concatenate(pieces, axis=0), 0.0)
+    qt = w.q_t[here, :]
+    lane = lanes((16, 128))
     for axis in range(3):
         offset = qt[:, axis : axis + 1] - w.k_row[axis : axis + 1, :]
         moved = jnp.sum(strength * offset, axis=1, keepdims=True) * (1.0 / w.atoms)
-        out = jnp.where(lane == axis, moved, out)
-    for s in range(16):
-        w.dis_s[s] = out[4 * s : 4 * s + 4]
+        stat = jnp.where(lane == 64 + axis, moved, stat)
+    for s in range(4):
+        w.lse_s[4 * q + s] = stat[4 * s : 4 * s + 4]
 
 
 def combine_attended(w):
@@ -217,12 +186,12 @@
 
 
 def combine_moved(w):
-    total = w.dis_r[0]
+    total = w.lse_r[0]
     for s in range(1, 16):
-        total = total + w.dis_r[s]
+        total = total + w.lse_r[s]
     w.pad[0:4, :] = total
     w.pad_t[...] = w.pad[...].T
-    return w.coords[...] + w.pad_t[0:3, 0:4]
+    return w.coords[...] + w.pad_t[64:67, 0:4]
 
 
 LOADED = dict(
@@ -253,13 +222,12 @@
     q_t=((64, 128), F32),
     k_row=((8, 128), F32),
     expanded=((64, 128), F32),
-    logits=((4096, 128), F32),
+    logits=((4, 1024, 128), F32),
     q_f=((64, 640), F32),
     k_f=((128, 640), F32),
     q_p=((64, 512), BF16),
     k_p=((128, 512), BF16),
     v_p=((128, 512), BF16),
-    strength=((64, 128), F32),
     coef=((64, 128), F32),
     pad=((128, 128), F32),
     pad_t=((128, 128), F32),
@@ -268,10 +236,8 @@
     k_nodes=((32, 4, 640), BF16),
     att_s=((16, 4, 512), BF16),
     lse_s=((16, 4, 128), F32),
-    dis_s=((16, 4, 128), F32),
     att_r=((16, 4, 512), BF16),
     lse_r=((16, 4, 128), F32),
-    dis_r=((16, 4, 128), F32),
 )
 
 
@@ -301,8 +267,8 @@
     refs = refs[2:]
     for name, ref in zip([*LOADED, *WORK], refs):
         setattr(w, name, ref)
-    load_sem, kz_send, kz_recv, kx_send, kx_recv, qn_send, qn_recv = refs[-13:-6]
-    at_send, at_recv, ls_send, ls_recv, ds_send, ds_recv = refs[-6:]
+    load_sem, kz_send, kz_recv, kx_send, kx_recv, qn_send, qn_recv = refs[-11:-4]
+    at_send, at_recv, ls_send, ls_recv = refs[-4:]
     w.atoms = float(rows * cols * 4)
     row, col = lax.axis_index("row"), lax.axis_index("col")
     x, line = lax.rem(row, 4), lax.rem(row // 4, 2)
@@ -349,10 +315,9 @@
     for n, (name, source) in enumerate(zip(LOADED, sources, strict=True)):
         loads.append(pltpu.make_async_copy(source, getattr(w, name), load_sem.at[n]))
         loads[-1].start()
-    for load in loads[:-2]:
+    for load in loads[:5]:
         load.wait()
     own_block(w)
-    prepare(w)
 
     pl.semaphore_wait(
         barrier, cols - 1 + planes - jnp.where(own_key, 1, 0) + jnp.where(relay, 3, 0)
@@ -432,6 +397,10 @@
     def _():
         w.k_nodes[half * cols + col] = w.own[...]
 
+    for load in loads[5:-2]:
+        load.wait()
+    prepare(w)
+
     @pl.when(relay)
     def _():
         def forward(n, carry):
@@ -463,21 +432,39 @@
             lax.fori_loop(0, cols // 2, arrive, 0)
 
     pair_distances(w)
-    geometry(w)
     for load in loads[-2:]:
         load.wait()
     project(w)
-    attention(w)
-    att = lambda c: w.att_s.at[c]
-    lse = lambda c: w.lse_s.at[c]
-    dis = lambda c: w.dis_s.at[c]
-    row_copies(att, w.att_r, at_send, at_recv, start)
-    row_copies(lse, w.lse_r, ls_send, ls_recv, start)
+
+    def out_copy(src, dst, send, recv, c):
+        return pltpu.make_async_remote_copy(
+            src_ref=src.at[c],
+            dst_ref=dst.at[col],
+            send_sem=send.at[c],
+            recv_sem=recv.at[col],
+            device_id=(row, c),
+            device_id_type=MESH,
+        )
+
+    def out_copies(q, src, dst, send, recv):
+        for s in range(4):
+            c = 4 * q + s
+
+            @pl.when(c != col)
+            def _(c=c):
+                out_copy(src, dst, send, recv, c).start()
+
+    mine = level // 2
+    far = mine // 2
+    for n, q in enumerate((3 - 3 * far, 2 - far, mine + 1 - 2 * lax.rem(mine, 2), mine)):
+        logits = w.logits.at[n]
+        geometry(w, q, logits)
+        stat = attention(w, q, logits)
+        out_copies(q, w.att_s, w.att_r, at_send, at_recv)
+        displacement(w, q, logits, stat)
+        out_copies(q, w.lse_s, w.lse_r, ls_send, ls_recv)
     w.att_r[col] = w.att_s[col]
     w.lse_r[col] = w.lse_s[col]
-    displacement(w)
-    row_copies(dis, w.dis_r, ds_send, ds_recv, start)
-    w.dis_r[col] = w.dis_s[col]
     far_copies(sent)
     row_copies(nod, w.q_nodes, qn_send, qn_recv, sent)
 
@@ -490,13 +477,18 @@
 
         lax.fori_loop(0, cols // 2, drain, 0)
 
-    row_copies(att, w.att_r, at_send, at_recv, sent)
-    row_copies(lse, w.lse_r, ls_send, ls_recv, sent)
-    wait_row(att, w.att_r, at_recv)
-    wait_row(lse, w.lse_r, ls_recv)
+    def finish(n, carry):
+        c = lax.rem(col + n, cols)
+        for src, dst, send, recv in (
+            (w.att_s, w.att_r, at_send, at_recv),
+            (w.lse_s, w.lse_r, ls_send, ls_recv),
+        ):
+            out_copy(src, dst, send, recv, c).wait_send()
+            pltpu.make_async_copy(src.at[c], dst.at[c], recv.at[c]).wait()
+        return carry
+
+    lax.fori_loop(1, cols, finish, 0)
     w.attended[...] = combine_attended(w)
-    row_copies(dis, w.dis_r, ds_send, ds_recv, sent)
-    wait_row(dis, w.dis_r, ds_recv)
     w.moved[...] = combine_moved(w)
 
 
@@ -534,7 +526,7 @@
         out_specs=(vmem, vmem),
         scratch_shapes=[pltpu.VMEM(*spec) for spec in [*LOADED.values(), *WORK.values()]]
         + [dma(len(LOADED)), dma(rows // 4), dma(cols), dma(3 * cols // 2), dma(cols)]
-        + [dma(cols)] * 8,
+        + [dma(cols)] * 6,
         compiler_params=pltpu.CompilerParams(collective_id=0, has_side_effects=True),
         name="refine",
     )(

time: 56.4 us -> 46.2 us (0.82)
  Pallas kernels: 53.1 us -> 42.8 us
    pallas_call x1, Pallas kernels: 53.1 us -> 42.8 us  [shards(): pl.pallas_call(functools.partial(kernel, rows, cols), out_shape=(jax.Shap...]
where the time goes in v2:
time: 46.2 us; the launch traced here: 46 us
  Pallas kernels  42.8 us (93%)
  local copies, waits for them, and re-layouts  2.5 us (5%)
  between operations  0.65 us (1%)
    pallas_call x1, Pallas kernels, shards(): pl.pallas_call(functools.partial(kernel, rows, cols), out_shape=(jax.Shap...  42.8 us
    unnamed x2, local copies, waits for them, and re-layouts  2.5 us

profile of v2, /device:TPU:1, one launch (start us, length us, event | category | flops | bytes accessed | tf_op | source)
XLA Modules:
  0.0 46.0 jit_solution(10829102398385742033)
XLA Ops:
  0.6 42.8 %refine.1 = (bf16[4,512]{1,0:T(4,128)(2,1)}, f32[3,4]{1,0:T(4,128)}) custom-call(bf16[4,512]{1,0:T(4,128)(2,1)} %refs_0_.1, f32[3,4]{1,0:T(4,128)} %refs_1_.1, s32[1,4]{1,0:T(1,128)} %bitcast.9, s32[1,4]{1,0:T(1,128)} %bitcast.10, f32[1,512]{1,0:T(1,128)} %bitcast.8, f32[1,128]{1,0:T(1,128)} %bitcast.11, f32[1,128]{1,0:T(1,128)} %bitcast.12, ...), custom_call_target="tpu_custom_call" | custom-call | tf_op jit(solution)/shard_map/refine/pallas_call | solution.py:519
  43.5 1.3 %copy.20 = bf16[4,512]{1,0:T(4,128)(2,1)} copy(bf16[4,512]{1,0:T(4,128)(2,1)} %get-tuple-element.4) | data formatting | bytes 8192
  44.7 1.2 %copy.21 = f32[3,4]{1,0:T(4,128)} copy(f32[3,4]{1,0:T(4,128)} %get-tuple-element.5) | data formatting | bytes 96

commit v3 on v2

--- a/solution.py
+++ b/solution.py
@@ -335,11 +335,12 @@
         )
 
     def far_copies(act):
-        def one(n, carry):
+        for n in [*range(planes // 2 + 1, 0, -2), *range(planes - 1, planes // 2 + 1, -2)]:
             act(far_copy(n))
-            return carry
-
-        lax.fori_loop(1, planes, one, 0)
+        for n in range(planes // 2, 0, -2):
+            act(far_copy(n))
+        for n in range(planes - 2, planes // 2, -2):
+            act(far_copy(n))
 
         @pl.when(jnp.logical_not(own_key))
         def _():
@@ -357,7 +358,7 @@
         )
 
     def row_copy(src, dst, send, recv, n):
-        c = lax.rem(col + n, cols)
+        c = lax.rem(col + cols - n, cols)
         return pltpu.make_async_remote_copy(
             src_ref=src(c),
             dst_ref=dst.at[col],
@@ -404,7 +405,9 @@
     @pl.when(relay)
     def _():
         def forward(n, carry):
-            pair = lax.rem(level + 1 + n, cols // 2)
+            m = jnp.where(line == lax.rem(level, 2), n, cols // 2 - 1 - n)
+            shift = (m + 1) // 2 * (2 * lax.rem(m, 2) - 1)
+            pair = lax.rem(level + shift + cols // 2, cols // 2)
             for side in range(2):
                 c = 2 * pair + side
 
@@ -490,6 +493,11 @@
     lax.fori_loop(1, cols, finish, 0)
     w.attended[...] = combine_attended(w)
     w.moved[...] = combine_moved(w)
+
+
+def hand_over(attended_from, moved_from, attended, moved):
+    attended[...] = attended_from[...]
+    moved[...] = moved_from[...]
 
 
 def shards(
@@ -516,12 +524,13 @@
     vmem = pl.BlockSpec(memory_space=pltpu.VMEM)
     hbm = pl.BlockSpec(memory_space=pl.ANY)
     dma = lambda n: pltpu.SemaphoreType.DMA((n,))
-    return pl.pallas_call(
+    outs = (
+        jax.ShapeDtypeStruct(nodes.shape, BF16),
+        jax.ShapeDtypeStruct(coords.shape, F32),
+    )
+    results = pl.pallas_call(
         functools.partial(kernel, rows, cols),
-        out_shape=(
-            jax.ShapeDtypeStruct(nodes.shape, BF16),
-            jax.ShapeDtypeStruct(coords.shape, F32),
-        ),
+        out_shape=outs,
         in_specs=[hbm] * len(LOADED),
         out_specs=(vmem, vmem),
         scratch_shapes=[pltpu.VMEM(*spec) for spec in [*LOADED.values(), *WORK.values()]]
@@ -547,6 +556,13 @@
         w_qkv,
         pair_bias,
     )
+    return pl.pallas_call(
+        hand_over,
+        out_shape=outs,
+        in_specs=[vmem, vmem],
+        out_specs=(vmem, vmem),
+        name="hand_over",
+    )(*results)
 
 
 def solution(mesh):

time: 46.2 us -> 44.2 us (0.957)
  local copies, waits for them, and re-layouts: 2.5 us -> 0 us
  Pallas kernels: 42.8 us -> 43.4 us
    unnamed x2 -> x0, local copies, waits for them, and re-layouts: 2.5 us -> none
    pallas_call x1 -> x2, Pallas kernels: 42.8 us -> 43.4 us  [the longest x1 42.1 us: shards(): pl.pallas_call(functools.partial(kernel, rows, cols), out_shape=outs, in_...]
where the time goes in v3:
time: 44.2 us; the launch traced here: 44 us
  Pallas kernels  43.4 us (98%)
  between operations  0.64 us (1%)
    pallas_call x1, Pallas kernels, shards(): pl.pallas_call(functools.partial(kernel, rows, cols), out_shape=outs, in_...  42.1 us
    pallas_call x1, Pallas kernels, shards(): pl.pallas_call(hand_over, out_shape=outs, in_specs=[vmem, vmem], out_spec...  1.27 us

profile of v3, /device:TPU:1, one launch (start us, length us, event | category | flops | bytes accessed | tf_op | source)
XLA Modules:
  0.0 44.0 jit_solution(8148367858533133711)
XLA Ops:
  0.6 42.1 %refine.1 = (bf16[4,512]{1,0:T(4,128)(2,1)}, f32[3,4]{1,0:T(4,128)}) custom-call(bf16[4,512]{1,0:T(4,128)(2,1)} %refs_0_.1, f32[3,4]{1,0:T(4,128)} %refs_1_.1, s32[1,4]{1,0:T(1,128)} %bitcast.9, s32[1,4]{1,0:T(1,128)} %bitcast.10, f32[1,512]{1,0:T(1,128)} %bitcast.8, f32[1,128]{1,0:T(1,128)} %bitcast.11, f32[1,128]{1,0:T(1,128)} %bitcast.12, ...), custom_call_target="tpu_custom_call" | custom-call | tf_op jit(solution)/shard_map/refine/pallas_call | solution.py:531
  42.8 1.3 %hand_over.1 = (bf16[4,512]{1,0:T(4,128)(2,1)}, f32[3,4]{1,0:T(4,128)}) custom-call(bf16[4,512]{1,0:T(4,128)(2,1)} %get-tuple-element.4.attended_from, f32[3,4]{1,0:T(4,128)} %get-tuple-element.5.moved_from), custom_call_target="tpu_custom_call" | custom-call | tf_op jit(solution)/shard_map/hand_over/pallas_call | solution.py:559

commit v4 on v3

--- a/solution.py
+++ b/solution.py
@@ -19,8 +19,9 @@
 
 
 def gelu(x):
-    half = 0.5 * x
-    return half + half * jnp.tanh(x * (GELU_A + GELU_B * (x * x)))
+    x = x.astype(BF16)
+    half = x * BF16(0.5)
+    return half + half * jnp.tanh(x * (BF16(GELU_A) + BF16(GELU_B) * (x * x)))
 
 
 def nt_dot(a, b):
@@ -51,23 +52,33 @@
     w.w2_b[...] = jnp.where(own, jnp.broadcast_to(wide, (8, 512)), 0.0).astype(BF16)
     mean = jnp.broadcast_to(w.gauss_mean[...], (128, 128)).T
     width = jnp.broadcast_to(w.gauss_width[...], (128, 128)).T
-    slope = math.sqrt(0.5 * math.log2(math.e)) / width
+    slope = math.sqrt(0.5) / width
     w.g_a[...] = slope
     w.g_b[...] = slope * mean
-    w.g_c[...] = -jnp.log2(math.sqrt(2.0 * math.pi) * width)
+    w.g_c[...] = -jnp.log(math.sqrt(2.0 * math.pi) * width)
 
 
 def joined(parts):
     return parts + pltpu.roll(parts, 120, 1) + pltpu.roll(parts, 112, 1)
 
 
-def pair_distances(w):
+def query_side(w):
     for s in range(w.q_nodes.shape[0]):
         w.q_f[4 * s : 4 * s + 4, :] = w.q_nodes[s].astype(F32)
+    w.q_p[...] = nn_dot(w.q_f[:, 0:512].astype(BF16), w.w_qkv[:, 0:512]).astype(BF16)
+    qt = joined(w.q_f[:, 512:640])
+    w.q_t[...] = qt
+    kinds = w.gauss_mul.shape[0]
+    q_hot = (lanes((64, kinds)).astype(F32) == qt[:, 3:4]).astype(F32)
+    high = lax.Precision.HIGHEST
+    w.q_mul[...] = nn_dot(q_hot, w.gauss_mul[...], high)
+    w.q_add[...] = nn_dot(q_hot, w.gauss_add[...], high)
+
+
+def pair_distances(w):
     for s in range(w.k_nodes.shape[0]):
         w.k_f[4 * s : 4 * s + 4, :] = w.k_nodes[s].astype(F32)
-    qt = joined(w.q_f[:, 512:640])
-    w.q_t[...] = qt
+    qt = w.q_t[...]
     kt = joined(w.k_f[:, 512:640]).T
     w.k_row[...] = kt[0:8, :]
     total = root_shift
@@ -76,11 +87,10 @@
         total = total + offset * offset
     distance = jnp.sqrt(total)
     kinds = w.gauss_mul.shape[0]
-    q_hot = (lanes((64, kinds)).astype(F32) == qt[:, 3:4]).astype(F32)
     k_hot = (lax.broadcasted_iota(jnp.int32, (kinds, 128), 0).astype(F32) == kt[3:4, :]).astype(F32)
     high = lax.Precision.HIGHEST
-    scale = nn_dot(nn_dot(q_hot, w.gauss_mul[...], high), k_hot, high)
-    shift = nn_dot(nn_dot(q_hot, w.gauss_add[...], high), k_hot, high)
+    scale = nn_dot(w.q_mul[...], k_hot, high)
+    shift = nn_dot(w.q_add[...], k_hot, high)
     w.expanded[...] = scale * distance + shift
 
 
@@ -91,17 +101,15 @@
         pieces = []
         for i in range(8):
             t = a * rows[i : i + 1, :] - b
-            pieces.append(jnp.exp2(k - t * t).astype(BF16))
-        hidden = gelu(nn_dot(w.wg_t[...], jnp.concatenate(pieces, axis=1))).astype(BF16)
+            pieces.append(jnp.exp(k - t * t).astype(BF16))
+        hidden = gelu(nn_dot(w.wg_t[...], jnp.concatenate(pieces, axis=1)))
         geo = nn_dot(w.w_heads[...], hidden)
         for i in range(8):
             logits[pl.ds(8 * part + i, 64, stride=16), :] = geo[:, 128 * i : 128 * i + 128]
 
 
 def project(w):
-    qn = w.q_f[:, 0:512].astype(BF16)
     kn = w.k_f[:, 0:512].astype(BF16)
-    w.q_p[...] = nn_dot(qn, w.w_qkv[:, 0:512]).astype(BF16)
     w.k_p[...] = nn_dot(kn, w.w_qkv[:, 512:1024]).astype(BF16)
     w.v_p[...] = nn_dot(kn, w.w_qkv[:, 1024:1536]).astype(BF16)
 
@@ -111,6 +119,7 @@
     take = (w.mask[here, :] == 1)[None]
     lane = lanes((16, 128))
     own = [(lane >> 3) == head for head in range(16)]
+    keep = [jnp.where(o, 1.0, 0.0).astype(BF16) for o in own]
     ones = jnp.ones((128, 128), BF16)
     scale = 1.0 / math.sqrt(8.0)
     maxima = jnp.zeros((16, 128), F32)
@@ -118,8 +127,8 @@
     for g in range(4):
         cols = slice(128 * g, 128 * g + 128)
         rows = slice(256 * g, 256 * g + 256)
-        q_g = w.q_p[here, cols].astype(F32)
-        left = jnp.concatenate([jnp.where(o, q_g, 0.0).astype(BF16) for o in own], axis=0)
+        q_g = w.q_p[here, cols]
+        left = jnp.concatenate([q_g * k for k in keep], axis=0)
         bias = w.bias[16 * g : 16 * g + 16, here, :].astype(F32).reshape(256, 128)
         logit = bias + logits[rows, :] + nt_dot(left, w.k_p[:, cols]) * scale
         logits[rows, :] = logit
@@ -147,7 +156,7 @@
     pieces = []
     for part in range(2):
         parts = [logits[pl.ds(8 * part + i, 64, stride=16), :].astype(BF16) for i in range(8)]
-        mixed = gelu(nn_dot(w.w1_t[...], jnp.concatenate(parts, axis=1))).astype(BF16)
+        mixed = gelu(nn_dot(w.w1_t[...], jnp.concatenate(parts, axis=1)))
         stacked = jnp.concatenate([mixed[:, 128 * i : 128 * i + 128] for i in range(8)], axis=0)
         pieces.append(nn_dot(w.w2_b[...], stacked))
     strength = jnp.where(w.mask[here, :] == 1, jnp.concatenate(pieces, axis=0), 0.0)
@@ -220,6 +229,8 @@
     g_b=((128, 128), F32),
     g_c=((128, 128), F32),
     q_t=((64, 128), F32),
+    q_mul=((64, 60), F32),
+    q_add=((64, 60), F32),
     k_row=((8, 128), F32),
     expanded=((64, 128), F32),
     logits=((4, 1024, 128), F32),
@@ -423,6 +434,9 @@
         lax.fori_loop(0, cols // 2, forward, 0)
 
     wait_row(nod, w.q_nodes, qn_recv)
+    for load in loads[-2:]:
+        load.wait()
+    query_side(w)
     for side in range(2):
 
         @pl.when(jnp.logical_not(jnp.logical_and(relay, half == side)))
@@ -435,8 +449,6 @@
             lax.fori_loop(0, cols // 2, arrive, 0)
 
     pair_distances(w)
-    for load in loads[-2:]:
-        load.wait()
     project(w)
 
     def out_copy(src, dst, send, recv, c):
@@ -452,6 +464,9 @@
     def out_copies(q, src, dst, send, recv):
         for s in range(4):
             c = 4 * q + s
+            if q is not mine:
+                out_copy(src, dst, send, recv, c).start()
+                continue
 
             @pl.when(c != col)
             def _(c=c):

time: 44.2 us -> 43.4 us (0.982)
  Pallas kernels: 43.4 us -> 42.5 us
    pallas_call x1, Pallas kernels: 42.1 us -> 41.3 us  [shards(): pl.pallas_call(functools.partial(kernel, rows, cols), out_shape=outs, in_...]
where the time goes in v4:
time: 43.4 us; the launch traced here: 43.2 us
  Pallas kernels  42.5 us (98%)
  between operations  0.64 us (1%)
    pallas_call x1, Pallas kernels, shards(): pl.pallas_call(functools.partial(kernel, rows, cols), out_shape=outs, in_...  41.3 us
    pallas_call x1, Pallas kernels, shards(): pl.pallas_call(hand_over, out_shape=outs, in_specs=[vmem, vmem], out_spec...  1.27 us

profile of v4, /device:TPU:1, one launch (start us, length us, event | category | flops | bytes accessed | tf_op | source)
XLA Modules:
  0.0 43.2 jit_solution(2243651649156400215)
XLA Ops:
  0.6 41.3 %refine.1 = (bf16[4,512]{1,0:T(4,128)(2,1)}, f32[3,4]{1,0:T(4,128)}) custom-call(bf16[4,512]{1,0:T(4,128)(2,1)} %refs_0_.1, f32[3,4]{1,0:T(4,128)} %refs_1_.1, s32[1,4]{1,0:T(1,128)} %bitcast.9, s32[1,4]{1,0:T(1,128)} %bitcast.10, f32[1,512]{1,0:T(1,128)} %bitcast.8, f32[1,128]{1,0:T(1,128)} %bitcast.11, f32[1,128]{1,0:T(1,128)} %bitcast.12, ...), custom_call_target="tpu_custom_call" | custom-call | tf_op jit(solution)/shard_map/refine/pallas_call | solution.py:546
  41.9 1.3 %hand_over.1 = (bf16[4,512]{1,0:T(4,128)(2,1)}, f32[3,4]{1,0:T(4,128)}) custom-call(bf16[4,512]{1,0:T(4,128)(2,1)} %get-tuple-element.4.attended_from, f32[3,4]{1,0:T(4,128)} %get-tuple-element.5.moved_from), custom_call_target="tpu_custom_call" | custom-call | tf_op jit(solution)/shard_map/hand_over/pallas_call | solution.py:574
